TPU v7x, 32 devices: a whole 2x2x4 slice. The times are simulated.
32 devices in a mesh: src: 4 (over z), snk: 4 (over x, core), sub: 2 (over y).
Axes of the slice: x: 2, y: 2, z: 4, core: 2. Of those that a mesh axis runs over, the one named last changes fastest.
Arguments:
- peram: bfloat16 [4, 4, 2, 512, 512], P('src', 'snk', None, 'sub'), may hold values from -6 to 6
- elemental: bfloat16 [2, 512, 512], replicated, may hold values from -0.0078125 to 0.0078125
- spin_signs: int32 [4], replicated, may hold values from 0 to 1
- insertions: int32 [4], replicated, may hold values from 0 to 3
Outputs:
- peram_full: bfloat16 [4, 4, 2, 512, 512], P('src', 'snk', None, 'sub')
- contraction: float32 [4, 4, 2, 512, 512], P('src', 'snk', None, 'sub')
Inputs may be any that keep to these rules, and one draw needn't show every extreme that they name: `spin_signs`: one entry for each of the four spin blocks. `insertions`: insertion times may repeat.
All inputs are finite; a program needn't handle non-finite values.
Results may differ from a plain program's by a relative error of at most 0.0029.
Values may be sent and summed in bfloat16 or wider, within the bound.
No kernel may reach another device: no remote copies, remote signals or barrier semaphores. Data moves between devices by JAX's collectives and lax.ppermute only.
A program may use at most 64 MiB of HBM per device.

v0:
```python
import jax
import jax.numpy as jnp
from jax import lax
from jax.sharding import PartitionSpec as P


def broadcast(block, axis, owner):
    block = jnp.where(lax.axis_index(axis) == owner, block, jnp.zeros_like(block))
    return lax.psum(block, axis)


def complex_product(first, second):
    real_part = jnp.dot(first[0], second[0], preferred_element_type=jnp.float32) - jnp.dot(
        first[1], second[1], preferred_element_type=jnp.float32
    )
    imag_part = jnp.dot(first[0], second[1], preferred_element_type=jnp.float32) + jnp.dot(
        first[1], second[0], preferred_element_type=jnp.float32
    )
    return jnp.stack([real_part, imag_part], axis=0)


def local(peram, elemental, spin_signs, insertions):
    n_sub = lax.axis_size("sub")
    n_snk = lax.axis_size("snk")
    own = peram[0, 0]
    rows_half = own.shape[1]
    width = own.shape[2]
    signs = 1.0 - 2.0 * jnp.repeat(spin_signs.astype(jnp.float32), width // 4)
    half_index = lax.axis_index("sub")
    col_signs = lax.dynamic_slice_in_dim(signs, half_index * rows_half, rows_half)
    flip = signs[:, None] * col_signs[None, :]
    mirror_re = flip * own[0].astype(jnp.float32).T
    mirror_im = -flip * own[1].astype(jnp.float32).T
    mirrored = jnp.stack([mirror_re, mirror_im], axis=0).astype(jnp.bfloat16)
    piece_rows = width // (n_sub * n_snk)
    outgoing = mirrored.reshape(2, n_sub, n_snk, piece_rows, rows_half)
    outgoing = outgoing.transpose(2, 1, 0, 3, 4).reshape(n_snk * n_sub, 1, 2, piece_rows, rows_half)
    spread = lax.all_to_all(outgoing, ("snk", "sub"), split_axis=0, concat_axis=1, tiled=True)
    spread = spread.reshape(n_snk, n_sub, 2, piece_rows, rows_half)
    homed = lax.all_to_all(
        lax.all_to_all(spread, "src", split_axis=0, concat_axis=0, tiled=True),
        "snk",
        split_axis=0,
        concat_axis=3,
        tiled=True,
    )
    upper = homed[0].transpose(1, 2, 0, 3).reshape(2, rows_half, width)
    row_block = lax.axis_index("src")
    col_block = lax.axis_index("snk")
    full_half = jnp.where(row_block >= col_block, own, upper)
    payload = complex_product(full_half, elemental).astype(jnp.bfloat16)
    total = jnp.zeros((2, rows_half, width), jnp.float32)
    for index in range(insertions.shape[0]):
        moment = insertions[index]
        received = broadcast(payload, "snk", moment)
        halves = []
        for part in range(n_sub):
            halves.append(broadcast(full_half, ("src", "sub"), moment * n_sub + part))
        right = jnp.concatenate(halves, axis=1)
        total = total + complex_product(received, right)
    return (full_half[None, None], total[None, None])


def solution(mesh):
    return jax.shard_map(
        local,
        mesh=mesh,
        in_specs=(P("src", "snk", None, "sub", None), P(), P(), P()),
        out_specs=(P("src", "snk", None, "sub", None), P("src", "snk", None, "sub", None)),
        check_vma=False,
    )
```

profile of v0, /device:TPU:0, one launch (start us, length us, event | category | flops | bytes accessed | tf_op | source)
XLA Modules:
  0.0 285.5 jit_solution(458601436078374853)
XLA Ops:
  7.2 1.2 copy.28
  8.9 13.8 %all_to_all.29 = bf16[8,1,2,64,256]{4,3,2,1,0:T(8,128)(2,1)S(1)} all-to-all(bf16[8,1,2,64,256]{4,3,2,1,0:T(8,128)(2,1)S(1)} %bitcast.150), channel_id=1, replica_groups=mesh['src'=4,'snk'=4,'sub'=2] {'snk','sub'}, dimensions={0} | all-to-all | bytes 1048576 | tf_op jit(solution)/shard_map/all_to_all | solution.py:38
  22.7 19.8 %all_to_all.30 = bf16[4,2,2,64,256]{4,3,2,1,0:T(8,128)(2,1)} all-to-all(bf16[4,2,2,64,256]{4,3,2,1,0:T(8,128)(2,1)S(1)} %bitcast.151), channel_id=1, replica_groups=mesh['src'=4,'snk'=4,'sub'=2] {'src'}, dimensions={0} | all-to-all | bytes 1048576 | tf_op jit(solution)/shard_map/all_to_all | solution.py:41
  42.5 3.5 %all-to-all-start.2 = ((bf16[4,2,2,64,256]{4,3,2,1,0:T(8,128)(2,1)}), bf16[4,2,2,64,256]{4,3,2,1,0:T(8,128)(2,1)S(1)}, u32[]{:S(2)}, u32[]{:S(2)}) async-start(bf16[4,2,2,64,256]{4,3,2,1,0:T(8,128)(2,1)} %all_to_all.30), calls=%async_computation.2 | async-start | bytes 1048576 | tf_op jit(solution)/shard_map/all_to_all | solution.py:40
  46.0 0.6 copy-done.13
  46.7 0.7 fusion.35
  50.0 4.8 %all-to-all-done.2 = bf16[4,2,2,64,256]{4,3,2,1,0:T(8,128)(2,1)S(1)} async-done(((bf16[4,2,2,64,256]{4,3,2,1,0:T(8,128)(2,1)}), bf16[4,2,2,64,256]{4,3,2,1,0:T(8,128)(2,1)S(1)}, u32[]{:S(2)}, u32[]{:S(2)}) %all-to-all-start.2) | async-done | bytes 524320 | tf_op jit(solution)/shard_map/all_to_all | solution.py:40
  54.9 1.0 copy-done.5
  55.9 0.9 broadcast_select_fusion
  56.7 1.9 broadcast_select_fusion.1
  62.5 1.4 broadcast_select_fusion.2
  64.2 1.0 copy.30
  65.2 147.6 %all-reduce.5.cloned.1.call-done = (bf16[2,256,512]{2,1,0:T(8,128)(2,1)}, bf16[2,256,512]{2,1,0:T(8,128)(2,1)}, bf16[2,256,512]{2,1,0:T(8,128)(2,1)}, bf16[2,256...) async-done(((bf16[2,256,512]{2,1,0:T(8,128)(2,1)}, ...) | async-done | bytes 4194320 | tf_op jit(solution)/shard_map/psum | solution.py:9
  212.8 1.1 constant_dynamic-update-slice_fusion.1
  214.1 1.0 copy-done.11
  215.3 50.5 %all-reduce.7.cloned.1.call-done = (bf16[2,256,512]{2,1,0:T(8,128)(2,1)}, bf16[2,256,512]{2,1,0:T(8,128)(2,1)}, bf16[2,256,512]{2,1,0:T(8,128)(2,1)}, bf16[2,256,512]{2,1,0:T(8,128)(2,1)}) async-done(((bf16[2,256,512]{2,1,0:T(8,128)(2,1)}, bf16[2,256,512]{2,1,0:T(8,128)(2,1)}, bf16[2,256,512]{2,1,0:T(8,128)(2,1)}, bf16[2,256,512]{2,1,0:T(8,128)(2,1)}), (bf16[2,256,512]{2,1,0:T(8,128)(2,1)}, ...) | async-done | bytes 2097168 | tf_op jit(solution)/shard_map/psum | solution.py:9
  265.8 1.3 fusion.24
  267.4 0.7 copy-done.3
  268.8 0.7 copy-done.7
  269.5 1.0 copy-done.6
  270.6 1.0 copy-done.9
  271.8 0.9 copy-done.2
  273.4 0.7 copy-done.1
  277.2 1.5 fusion.13
  (59 shorter events, 7.2 us)
Async XLA Ops:
  7.2 1.3 copy-start.14
  42.5 12.3 %all-to-all-start.2 = ((bf16[4,2,2,64,256]{4,3,2,1,0:T(8,128)(2,1)}), bf16[4,2,2,64,256]{4,3,2,1,0:T(8,128)(2,1)S(1)}, u32[]{:S(2)}, u32[]{:S(2)}) async-start(bf16[4,2,2,64,256]{4,3,2,1,0:T(8,128)(2,1)} %all_to_all.30), calls=%async_computation.2 | async-start | bytes 1048576 | tf_op jit(solution)/shard_map/all_to_all | solution.py:40
  46.0 166.9 %all-reduce.5.cloned.1.call-start = ((), (), s32[]{:S(2)}) async-start(), calls=%async_computation.3 | async-start | bytes 8388608 | tf_op jit(solution)/shard_map/psum | solution.py:9
  46.0 0.7 copy-start.13
  54.8 1.0 copy-start.5
  58.6 2.7 copy-start
  58.6 207.2 %all-reduce.7.cloned.1.call-start = ((), (), s32[]{:S(2)}) async-start(), calls=%async_computation.4 | async-start | bytes 4194304 | tf_op jit(solution)/shard_map/psum | solution.py:9
  212.8 1.2 copy-start.8
  214.0 1.0 copy-start.11
  214.0 1.2 copy-start.12
  265.8 1.3 copy-start.4
  267.1 1.0 copy-start.3
  268.4 1.0 copy-start.7
  269.5 1.0 copy-start.6
  270.5 1.0 copy-start.9
  270.5 1.2 copy-start.10
  271.7 1.0 copy-start.2
  273.1 1.0 copy-start.1
Sparse Core Ops, SparseCore 0:
  58.7 154.0 all-reduce.4
  215.4 50.3 all-reduce.6
where the time goes:
time: 286 us; the launch traced here: 285 us
  waiting for transfers between devices  203 us (71%)
  blocking collectives  33.6 us (12%)
  between operations  19.7 us (7%)
  local copies, waits for them, and re-layouts  13 us (5%)
  matrix products  6.95 us (2%)
  other arithmetic  5.86 us (2%)
  starting transfers between devices  3.55 us (1%)
    psum x2, waiting for transfers between devices, broadcast(): return lax.psum(block, axis)  198 us
    all_to_all x1, blocking collectives, local(): lax.all_to_all(spread, 'src', split_axis=0, concat_axis=0, tiled=True)  19.8 us
    all_to_all x1, blocking collectives, local(): lax.all_to_all(outgoing, ('snk', 'sub'), split_axis=0, concat_axis=1, til...  13.8 us
    unnamed x36, local copies, waits for them, and re-layouts  11.7 us
  transfers between devices with their start and end apart: 3, of which 3 were waited for; matrix products, arithmetic and copies ran while one was open for 2% of the time, Pallas kernels for 0%

commit v1 on v0

--- a/solution.py
+++ b/solution.py
@@ -3,10 +3,14 @@
 from jax import lax
 from jax.sharding import PartitionSpec as P
 
+_balance_state = lambda body, bus_axis: jnp.sum(
+    jax.lax.all_gather(body, axis_name=bus_axis), axis=0
+)
+
 
 def broadcast(block, axis, owner):
     block = jnp.where(lax.axis_index(axis) == owner, block, jnp.zeros_like(block))
-    return lax.psum(block, axis)
+    return _balance_state(block, axis)
 
 
 def complex_product(first, second):

time: 286 us -> 759 us (2.65)
  waiting for transfers between devices: 203 us -> 636 us
  other arithmetic: 5.86 us -> 42.5 us
  matrix products: 6.95 us -> 17.5 us
  local copies, waits for them, and re-layouts: 13 us -> 4.22 us
    all_gather x0 -> x12, waiting for transfers between devices: none -> 625 us  [jax.lax.all_gather(body, axis_name=bus_axis)]
    psum x2 -> x0, waiting for transfers between devices: 198 us -> none  [broadcast(): return lax.psum(block, axis)]
    reduce_sum x0 -> x12, other arithmetic: none -> 35.8 us  [jnp.sum(jax.lax.all_gather(body, axis_name=bus_axis), axis=0)]
    unnamed x36, local copies, waits for them, and re-layouts: 11.7 us -> 2.32 us
  transfers between devices with their start and end apart: 3 -> 13, of which waited for: 3 -> 13; matrix products, arithmetic and copies ran while one was open for 2% -> 6% of each run, Pallas kernels for 0% -> 0%
where the time goes in v1:
time: 759 us; the launch traced here: 758 us
  waiting for transfers between devices  636 us (84%)
  other arithmetic  42.5 us (6%)
  blocking collectives  33.7 us (4%)
  between operations  19.5 us (3%)
  matrix products  17.5 us (2%)
    all_gather x12, waiting for transfers between devices, jax.lax.all_gather(body, axis_name=bus_axis)  625 us
    reduce_sum x12, other arithmetic, jnp.sum(jax.lax.all_gather(body, axis_name=bus_axis), axis=0)  35.8 us
    all_to_all x1, blocking collectives, local(): lax.all_to_all(spread, 'src', split_axis=0, concat_axis=0, tiled=True)  19.8 us
  transfers between devices with their start and end apart: 13, of which 13 were waited for; matrix products, arithmetic and copies ran while one was open for 6% of the time, Pallas kernels for 0%

profile of v1, /device:TPU:0, one launch (start us, length us, event | category | flops | bytes accessed | tf_op | source)
XLA Modules:
  0.0 757.7 jit_solution(4344423147505105243)
XLA Ops:
  9.5 13.9 %all_to_all.29 = bf16[8,1,2,64,256]{4,3,2,1,0:T(8,128)(2,1)S(1)} all-to-all(bf16[8,1,2,64,256]{4,3,2,1,0:T(8,128)(2,1)S(1)} %bitcast.152), channel_id=1, replica_groups=mesh['src'=4,'snk'=4,'sub'=2] {'snk','sub'}, dimensions={0} | all-to-all | bytes 1048576 | tf_op jit(solution)/shard_map/all_to_all | solution.py:42
  23.5 19.8 %all_to_all.30 = bf16[4,2,2,64,256]{4,3,2,1,0:T(8,128)(2,1)} all-to-all(bf16[4,2,2,64,256]{4,3,2,1,0:T(8,128)(2,1)S(1)} %bitcast.153), channel_id=1, replica_groups=mesh['src'=4,'snk'=4,'sub'=2] {'src'}, dimensions={0} | all-to-all | bytes 1048576 | tf_op jit(solution)/shard_map/all_to_all | solution.py:45
  43.3 3.5 all-to-all-start.2
  49.8 5.7 all-to-all-done.2
  72.1 6.5 all-gather.31.cloned.1.call-done
  81.5 21.3 %all-gather.19.cloned.1.call-done = bf16[4,2,256,512]{3,2,1,0:T(8,128)(2,1)} async-done(((bf16[1,2,256,512]{3,2,1,0:T(8,128)(2,1)}), bf16[4,2,256,512]{3,2,1,0:T(8,128)(2,1)}) %all-gather.19.cloned.1.call-update) | async-done | bytes 2097168 | tf_op jit(solution)/shard_map/all_gather | solution.py:7
  105.6 21.3 %all-gather.25.cloned.1.call-done = bf16[4,2,256,512]{3,2,1,0:T(8,128)(2,1)} async-done(((bf16[1,2,256,512]{3,2,1,0:T(8,128)(2,1)}), bf16[4,2,256,512]{3,2,1,0:T(8,128)(2,1)}) %all-gather.25.cloned.1.call-update) | async-done | bytes 2097168 | tf_op jit(solution)/shard_map/all_gather | solution.py:7
  129.8 21.2 %all-gather.13.cloned.1.call-done = bf16[4,2,256,512]{3,2,1,0:T(8,128)(2,1)} async-done(((bf16[1,2,256,512]{3,2,1,0:T(8,128)(2,1)}), bf16[4,2,256,512]{3,2,1,0:T(8,128)(2,1)}) %all-gather.13.cloned.1.call-update) | async-done | bytes 2097168 | tf_op jit(solution)/shard_map/all_gather | solution.py:7
  153.8 71.9 %all-gather.33.cloned.1.call-done = bf16[8,2,256,512]{3,2,1,0:T(8,128)(2,1)} async-done(((bf16[1,2,256,512]{3,2,1,0:T(8,128)(2,1)}), bf16[8,2,256,512]{3,2,1,0:T(8,128)(2,1)}) %all-gather.33.cloned.1.call-update) | async-done | bytes 4194320 | tf_op jit(solution)/shard_map/all_gather | solution.py:7
  225.7 3.0 reduce_sum.154
  228.7 70.4 %all-gather.29.cloned.1.call-done = bf16[8,2,256,512]{3,2,1,0:T(8,128)(2,1)} async-done(((bf16[1,2,256,512]{3,2,1,0:T(8,128)(2,1)}), bf16[8,2,256,512]{3,2,1,0:T(8,128)(2,1)}) %all-gather.29.cloned.1.call-update) | async-done | bytes 4194320 | tf_op jit(solution)/shard_map/all_gather | solution.py:7
  299.1 3.0 reduce_sum.152
  302.0 70.5 %all-gather.27.cloned.1.call-done = bf16[8,2,256,512]{3,2,1,0:T(8,128)(2,1)} async-done(((bf16[1,2,256,512]{3,2,1,0:T(8,128)(2,1)}), bf16[8,2,256,512]{3,2,1,0:T(8,128)(2,1)}) %all-gather.27.cloned.1.call-update) | async-done | bytes 4194320 | tf_op jit(solution)/shard_map/all_gather | solution.py:7
  372.6 3.0 reduce_sum.151
  375.5 70.5 %all-gather.23.cloned.1.call-done = bf16[8,2,256,512]{3,2,1,0:T(8,128)(2,1)} async-done(((bf16[1,2,256,512]{3,2,1,0:T(8,128)(2,1)}), bf16[8,2,256,512]{3,2,1,0:T(8,128)(2,1)}) %all-gather.23.cloned.1.call-update) | async-done | bytes 4194320 | tf_op jit(solution)/shard_map/all_gather | solution.py:7
  446.0 3.0 reduce_sum.149
  449.0 70.5 %all-gather.21.cloned.1.call-done = bf16[8,2,256,512]{3,2,1,0:T(8,128)(2,1)} async-done(((bf16[1,2,256,512]{3,2,1,0:T(8,128)(2,1)}), bf16[8,2,256,512]{3,2,1,0:T(8,128)(2,1)}) %all-gather.21.cloned.1.call-update) | async-done | bytes 4194320 | tf_op jit(solution)/shard_map/all_gather | solution.py:7
  519.5 3.0 reduce_sum.148
  522.5 70.4 %all-gather.17.cloned.1.call-done = bf16[8,2,256,512]{3,2,1,0:T(8,128)(2,1)} async-done(((bf16[1,2,256,512]{3,2,1,0:T(8,128)(2,1)}), bf16[8,2,256,512]{3,2,1,0:T(8,128)(2,1)}) %all-gather.17.cloned.1.call-update) | async-done | bytes 4194320 | tf_op jit(solution)/shard_map/all_gather | solution.py:7
  592.9 3.0 reduce_sum.146
  595.8 70.5 %all-gather.15.cloned.1.call-done = bf16[8,2,256,512]{3,2,1,0:T(8,128)(2,1)} async-done(((bf16[1,2,256,512]{3,2,1,0:T(8,128)(2,1)}), bf16[8,2,256,512]{3,2,1,0:T(8,128)(2,1)}) %all-gather.15.cloned.1.call-update) | async-done | bytes 4194320 | tf_op jit(solution)/shard_map/all_gather | solution.py:7
  666.4 3.7 reduce_sum.145
  679.9 59.8 %all-gather.35.cloned.1.call-done = bf16[8,2,256,512]{3,2,1,0:T(8,128)(2,1)} async-done(((bf16[1,2,256,512]{3,2,1,0:T(8,128)(2,1)}), bf16[8,2,256,512]{3,2,1,0:T(8,128)(2,1)}) %all-gather.35.cloned.1.call-update) | async-done | bytes 4194320 | tf_op jit(solution)/shard_map/all_gather | solution.py:7
  739.7 3.0 reduce_sum.155
  (101 shorter events, 46.1 us)
Async XLA Ops:
  7.2 39.6 %copy-start.16 = (s32[4]{0:T(128)S(1)}, s32[4]{0:T(128)}, u32[]{:S(2)}) copy-start(s32[4]{0:T(128)} %param.7) | copy-start | bytes 52
  9.5 46.4 %copy-start.3 = (bf16[2,512,512]{2,1,0:T(8,128)(2,1)S(1)}, bf16[2,512,512]{2,1,0:T(8,128)(2,1)}, u32[]{:S(2)}) copy-start(bf16[2,512,512]{2,1,0:T(8,128)(2,1)} %param.5) | copy-start | bytes 3145732
  43.3 12.3 %all-to-all-start.2 = ((bf16[4,2,2,64,256]{4,3,2,1,0:T(8,128)(2,1)}), bf16[4,2,2,64,256]{4,3,2,1,0:T(8,128)(2,1)S(1)}, u32[]{:S(2)}, u32[]{:S(2)}) async-start(bf16[4,2,2,64,256]{4,3,2,1,0:T(8,128)(2,1)} %all_to_all.30), calls=%async_computation.2 | async-start | bytes 1048576 | tf_op jit(solution)/shard_map/all_to_all | solution.py:44
  46.8 31.9 %all-gather.31.cloned.1.call-start = ((), (), s32[]{:S(2)}) async-start(), calls=%async_computation.12 | async-start | bytes 2621440 | tf_op jit(solution)/shard_map/all_gather | solution.py:7
  56.9 5.4 copy-start.12
  58.6 44.2 %all-gather.19.cloned.1.call-start = ((), (), s32[]{:S(2)}) async-start(), calls=%async_computation.6 | async-start | bytes 2621440 | tf_op jit(solution)/shard_map/all_gather | solution.py:7
  59.4 67.6 %all-gather.25.cloned.1.call-start = ((), (), s32[]{:S(2)}) async-start(), calls=%async_computation.9 | async-start | bytes 2621440 | tf_op jit(solution)/shard_map/all_gather | solution.py:7
  60.1 90.8 %all-gather.13.cloned.1.call-start = ((), (), s32[]{:S(2)}) async-start(), calls=%async_computation.3 | async-start | bytes 2621440 | tf_op jit(solution)/shard_map/all_gather | solution.py:7
  60.7 165.1 %all-gather.33.cloned.1.call-start = ((), (), s32[]{:S(2)}) async-start(), calls=%async_computation.13 | async-start | bytes 4718592 | tf_op jit(solution)/shard_map/all_gather | solution.py:7
  63.2 235.9 %all-gather.29.cloned.1.call-start = ((), (), s32[]{:S(2)}) async-start(), calls=%async_computation.11 | async-start | bytes 4718592 | tf_op jit(solution)/shard_map/all_gather | solution.py:7
  66.9 305.6 %all-gather.27.cloned.1.call-start = ((), (), s32[]{:S(2)}) async-start(), calls=%async_computation.10 | async-start | bytes 4718592 | tf_op jit(solution)/shard_map/all_gather | solution.py:7
  67.7 378.4 %all-gather.23.cloned.1.call-start = ((), (), s32[]{:S(2)}) async-start(), calls=%async_computation.8 | async-start | bytes 4718592 | tf_op jit(solution)/shard_map/all_gather | solution.py:7
  68.4 451.1 %all-gather.21.cloned.1.call-start = ((), (), s32[]{:S(2)}) async-start(), calls=%async_computation.7 | async-start | bytes 4718592 | tf_op jit(solution)/shard_map/all_gather | solution.py:7
  69.2 523.7 %all-gather.17.cloned.1.call-start = ((), (), s32[]{:S(2)}) async-start(), calls=%async_computation.5 | async-start | bytes 4718592 | tf_op jit(solution)/shard_map/all_gather | solution.py:7
  69.7 596.6 %all-gather.15.cloned.1.call-start = ((), (), s32[]{:S(2)}) async-start(), calls=%async_computation.4 | async-start | bytes 4718592 | tf_op jit(solution)/shard_map/all_gather | solution.py:7
  70.5 669.2 %all-gather.35.cloned.1.call-start = ((), (), s32[]{:S(2)}) async-start(), calls=%async_computation.14 | async-start | bytes 4718592 | tf_op jit(solution)/shard_map/all_gather | solution.py:7
  595.8 78.6 %copy-start = (bf16[2,256,512]{2,1,0:T(8,128)(2,1)}, bf16[2,256,512]{2,1,0:T(8,128)(2,1)S(1)}, u32[]{:S(2)}) copy-start(bf16[2,256,512]{2,1,0:T(8,128)(2,1)S(1)} %reduce_sum.146) | copy-start | bytes 1572868
  670.1 6.5 copy-start.7
  670.1 7.6 copy-start.5
  742.7 4.5 copy-start.1
  742.7 4.5 copy-start.2
  742.7 4.5 copy-start.9
  742.7 4.8 copy-start.8
  742.7 4.8 copy-start.11
  (6 other events, 16.2 us)
Sparse Core Ops, SparseCore 0:
  58.7 19.8 all-gather.30
  80.2 22.5 all-gather.18
  104.3 22.5 all-gather.24
  128.3 22.5 all-gather.12
  152.9 72.7 all-gather.32
  227.7 71.3 all-gather.28
  301.2 71.3 all-gather.26
  374.7 71.3 all-gather.22
  448.2 71.3 all-gather.20
  521.5 71.3 all-gather.16
  595.0 71.3 all-gather.14
  668.3 71.3 all-gather.34
